TPU v7x, 32 devices: a whole 2x2x4 slice. The times are simulated.
32 devices in a mesh: freq: 4 (over y, x), space: 8 (over z, core).
Axes of the slice: x: 2, y: 2, z: 4, core: 2. Of those that a mesh axis runs over, the one named last changes fastest.
Arguments:
- spectra: bfloat16 [2, 256, 24, 32768], P(None, 'freq', None, 'space'), may hold values from -6 to 6
- eigvecs: bfloat16 [2, 256, 4, 32768], P(None, 'freq', None, 'space'), may hold values from -6 to 6
- weights: bfloat16 [32768], P('space'), may hold values from 0.19921875 to 5
Outputs:
- filtered: float32 [3200, 32768], P(None, ('space', 'freq'))
All inputs are finite; a program needn't handle non-finite values.
Results may differ from a plain program's by a relative error of at most 0.004.
Values may be sent and summed in bfloat16 or wider, within the bound.
A program may use at most 128 MiB of HBM per device.

v0:
```python
import functools
import math

import jax
import jax.numpy as jnp
import numpy as np
from jax import lax
from jax.experimental import pallas as pl
from jax.experimental.pallas import tpu as pltpu
from jax.sharding import PartitionSpec as P

MESH = pl.DeviceIdType.MESH
GROUP = 32


def project_kernel(blocks, group, modes_ref, spectra_ref, weights_ref, out_ref, acc_ref):
    step = pl.program_id(1)
    half = modes_ref.shape[2]
    weights = weights_ref[...].astype(jnp.float32)
    weighted = jnp.concatenate(
        [(modes_ref[0, c].astype(jnp.float32) * weights).astype(jnp.bfloat16) for c in range(2)], axis=0
    )
    owner = lax.broadcasted_iota(jnp.int32, (blocks, 2 * half), 1) % half // (half // group)

    @pl.when(step == 0)
    def _():
        acc_ref[...] = jnp.zeros_like(acc_ref)

    for c in range(2):
        product = lax.dot_general(
            spectra_ref[c], weighted, (((1,), (1,)), ((), ())), preferred_element_type=jnp.float32
        )
        total = acc_ref[c]
        for j in range(group):
            total += jnp.where(owner == j, product[j * blocks : (j + 1) * blocks], 0.0)
        acc_ref[c] = total

    @pl.when(step == pl.num_programs(1) - 1)
    def _():
        out_ref[0, 0] = acc_ref[0][:, :half] + acc_ref[1][:, half:]
        out_ref[0, 1] = acc_ref[1][:, :half] - acc_ref[0][:, half:]


def project(modes, spectra, weights, blocks, group, modes_count):
    parts, _, rows, width = modes.shape
    half = group * modes_count
    steps = rows // half
    points = spectra.shape[2]
    return pl.pallas_call(
        functools.partial(project_kernel, blocks, group),
        out_shape=jax.ShapeDtypeStruct((steps, 2, blocks, half), jnp.float32),
        grid=(steps, parts),
        in_specs=[
            pl.BlockSpec((1, 2, half, width), lambda h, i: (i, 0, h, 0)),
            pl.BlockSpec((2, group * blocks, width), lambda h, i: (0, h, i)),
            pl.BlockSpec((1, width), lambda h, i: (0, i)),
        ],
        out_specs=pl.BlockSpec((1, 2, blocks, half), lambda h, i: (h, 0, 0, 0)),
        scratch_shapes=[pltpu.VMEM((2, blocks, 2 * half), jnp.float32)],
        compiler_params=pltpu.CompilerParams(vmem_limit_bytes=48 << 20),
        cost_estimate=pl.CostEstimate(
            flops=4 * spectra.shape[1] * points * 2 * half,
            bytes_accessed=4 * spectra.shape[1] * points,
            transcendentals=0,
        ),
        name="project",
    )(modes, spectra, weights)


def exchange_kernel(n_freq, n_space, part_ref, out_ref, land, own, every, send1, recv1, send2, recv2):
    f = lax.axis_index("freq")
    s = lax.axis_index("space")
    peers = [(df, ds) for df in range(n_freq) for ds in range(n_space) if (df, ds) != (0, 0)]

    def at(df, ds):
        return (lax.rem(f + df, n_freq), lax.rem(s + ds, n_space))

    barrier = pltpu.get_barrier_semaphore()
    for df, ds in peers:
        pl.semaphore_signal(barrier, inc=1, device_id=at(df, ds), device_id_type=MESH)
    pl.semaphore_wait(barrier, len(peers))

    first = []
    for ds in range(1, n_space):
        target = at(0, ds)
        copy = pltpu.make_async_remote_copy(
            src_ref=part_ref.at[target[1]], dst_ref=land.at[ds],
            send_sem=send1.at[ds], recv_sem=recv1.at[ds],
            device_id=target, device_id_type=MESH,
        )
        copy.start()
        first.append(copy)
    total = part_ref[s]
    for ds in range(1, n_space):
        first[ds - 1].wait_recv()
        total += land[ds]
    own[...] = total
    second = []
    for df, ds in peers:
        copy = pltpu.make_async_remote_copy(
            src_ref=own, dst_ref=every.at[f, s],
            send_sem=send2.at[df * n_space + ds], recv_sem=recv2.at[df * n_space + ds],
            device_id=at(df, ds), device_id_type=MESH,
        )
        copy.start()
        second.append(copy)
    every[f, s] = total
    for copy in second:
        copy.wait_recv()
    out_ref[...] = every[...]
    for copy in first + second:
        copy.wait_send()


def exchange(part, n_freq, n_space):
    piece = part.shape[1:]
    return pl.pallas_call(
        functools.partial(exchange_kernel, n_freq, n_space),
        out_shape=jax.ShapeDtypeStruct((n_freq, n_space) + piece, jnp.float32),
        in_specs=[pl.BlockSpec(memory_space=pltpu.VMEM)],
        out_specs=pl.BlockSpec(memory_space=pltpu.VMEM),
        scratch_shapes=[
            pltpu.VMEM((n_space,) + piece, jnp.float32),
            pltpu.VMEM(piece, jnp.float32),
            pltpu.VMEM((n_freq, n_space) + piece, jnp.float32),
            pltpu.SemaphoreType.DMA((n_space,)),
            pltpu.SemaphoreType.DMA((n_space,)),
            pltpu.SemaphoreType.DMA((n_freq * n_space,)),
            pltpu.SemaphoreType.DMA((n_freq * n_space,)),
        ],
        compiler_params=pltpu.CompilerParams(collective_id=0, has_side_effects=True),
        cost_estimate=pl.CostEstimate(flops=1 << 20, bytes_accessed=24 << 20, transcendentals=0),
        name="exchange",
    )(part)


def synthesis_kernel(factor, coef_ref, modes_ref, basis_ref, out_ref, left_ref, mid_ref):
    groups, _, blocks, half = coef_ref.shape
    parts, _, rows, tile = modes_ref.shape
    chunk = 2 * GROUP
    length = groups * GROUP

    @pl.when(pl.program_id(0) == 0)
    def _():
        lane = lax.broadcasted_iota(jnp.int32, (GROUP, 2 * half), 1) % half // (half // GROUP)
        mask = lane == lax.broadcasted_iota(jnp.int32, (GROUP, 2 * half), 0)

        def fill(g, carry):
            real = coef_ref[g, 0] * factor
            imag = coef_ref[g, 1] * factor
            line_r = jnp.concatenate([real, -imag], axis=1)
            line_i = jnp.concatenate([imag, real], axis=1)
            for b in range(blocks):
                left_ref[g, b * chunk : b * chunk + GROUP] = jnp.where(
                    mask, line_r[b : b + 1], 0.0
                ).astype(jnp.bfloat16)
                left_ref[g, b * chunk + GROUP : (b + 1) * chunk] = jnp.where(
                    mask, line_i[b : b + 1], 0.0
                ).astype(jnp.bfloat16)
            return carry

        lax.fori_loop(0, groups, fill, 0)

    for g in range(groups):
        pieces = []
        for c in range(2):
            start = g * half
            stop = start + half
            while start < stop:
                p, r = divmod(start, rows)
                n = min(stop - start, rows - r)
                pieces.append(modes_ref[p, c, r : r + n])
                start += n
        modes = jnp.concatenate(pieces, axis=0)
        rebuilt = jnp.dot(left_ref[g], modes, preferred_element_type=jnp.float32).astype(jnp.bfloat16)
        for b in range(blocks):
            mid_ref[b, g * chunk : (g + 1) * chunk] = rebuilt[b * chunk : (b + 1) * chunk]

    step = length // 2
    carry = None
    for b in range(blocks):
        series = jnp.dot(basis_ref[...], mid_ref[b], preferred_element_type=jnp.float32)
        lead = series[:step]
        out_ref[b * step : (b + 1) * step] = lead if carry is None else lead + carry
        carry = series[step:]
    out_ref[blocks * step :] = carry


def synthesis(coefs, modes, factor):
    groups, _, blocks, half = coefs.shape
    parts, _, rows, columns = modes.shape
    length = groups * GROUP
    tile = 256 if columns % 256 == 0 else columns
    freq = np.arange(length).reshape(groups, 1, GROUP)
    time = np.arange(length).reshape(length, 1, 1, 1)
    phase = 2.0 * np.pi * ((freq * time) % length) / length
    both = np.concatenate([np.cos(phase), -np.sin(phase)], axis=2)
    window = np.sin(np.pi * (np.arange(length) + 0.5) / length) / math.sqrt(length)
    basis = jnp.asarray((both.reshape(length, 2 * length) * window[:, None]).astype(np.float32)).astype(jnp.bfloat16)
    out_rows = (blocks + 1) * (length // 2)
    return pl.pallas_call(
        functools.partial(synthesis_kernel, factor),
        out_shape=jax.ShapeDtypeStruct((out_rows, columns), jnp.float32),
        grid=(columns // tile,),
        in_specs=[
            pl.BlockSpec((groups, 2, blocks, half), lambda i: (0, 0, 0, 0)),
            pl.BlockSpec((parts, 2, rows, tile), lambda i: (0, 0, 0, i)),
            pl.BlockSpec((length, 2 * length), lambda i: (0, 0)),
        ],
        out_specs=pl.BlockSpec((out_rows, tile), lambda i: (0, i)),
        scratch_shapes=[
            pltpu.VMEM((groups, blocks * 2 * GROUP, 2 * half), jnp.bfloat16),
            pltpu.VMEM((blocks, 2 * length, tile), jnp.bfloat16),
        ],
        compiler_params=pltpu.CompilerParams(vmem_limit_bytes=56 << 20),
        cost_estimate=pl.CostEstimate(
            flops=8 * length * length * blocks * columns, bytes_accessed=4 * out_rows * columns, transcendentals=0
        ),
        name="synthesis",
    )(coefs, modes, basis)


def body(spectra, eigvecs, weights):
    n_freq = lax.axis_size("freq")
    n_space = lax.axis_size("space")
    _, count, blocks, points = spectra.shape
    modes_count = eigvecs.shape[2]
    factor = 1.0 / math.sqrt(points * n_space)
    group = min(GROUP, count)
    width = points // n_freq
    send = eigvecs.reshape(2, count * modes_count, n_freq, width).transpose(2, 0, 1, 3)
    moved = lax.all_to_all(send, "freq", split_axis=0, concat_axis=0, tiled=True)
    part = project(
        send, spectra.reshape(2, count * blocks, points), weights.reshape(1, points), blocks, group, modes_count
    )
    piece = part.size // n_space
    shape = (piece // 128, 128) if piece % 128 == 0 else (1, piece)
    coefs = exchange(part.reshape((n_space,) + shape), n_freq, n_space)
    half = group * modes_count
    joined = GROUP // group
    coefs = coefs.reshape(-1, joined, 2, blocks, half).transpose(0, 2, 3, 1, 4)
    coefs = coefs.reshape(-1, 2, blocks, joined * half)
    return synthesis(coefs, moved, factor)


def solution(mesh):
    placed = (P(None, "freq", None, "space"), P(None, "freq", None, "space"), P("space"))
    return jax.shard_map(
        body, mesh=mesh, in_specs=placed, out_specs=P(None, ("space", "freq")), check_vma=False
    )
```

profile of v0, /device:TPU:0, one launch (start us, length us, event | category | flops | bytes accessed | tf_op | source)
XLA Modules:
  0.0 102.6 jit_solution(17312016103555781837)
XLA Ops:
  0.0 7.8 %reshape.12 = bf16[2,256,4,1024]{3,2,1,0:T(4,128)(2,1)} reshape(bf16[2,64,4,4096]{3,2,1,0:T(4,128)(2,1)} %param.5) | data formatting | bytes 8388608 | tf_op jit(solution)/shard_map/reshape | solution.py:231
  7.8 5.5 %copy.7 = bf16[2,256,4,1024]{3,1,0,2:T(8,128)(2,1)} copy(bf16[2,256,4,1024]{3,2,1,0:T(4,128)(2,1)} %reshape.12) | data formatting | bytes 8388608 | tf_op jit(solution)/shard_map/reshape | solution.py:231
  13.4 0.0 copy-start.1
  13.4 5.3 %all-to-all-start = ((bf16[4,2,256,1024]{3,2,1,0:T(8,128)(2,1)}), bf16[4,2,256,1024]{3,2,1,0:T(8,128)(2,1)}, u32[]{:S(2)}, u32[]{:S(2)}) async-start(bf16[4,2,256,1024]{3,2,1,0:T(8,128)(2,1)} %bitcast.6), calls=%async_computation | async-start | bytes 8388608 | tf_op jit(solution)/shard_map/all_to_all | solution.py:232
  18.7 0.0 copy-done.1
  18.7 0.0 copy-start
  18.7 2.2 %copy-done = bf16[2,256,4,1024]{3,1,0,2:T(8,128)(2,1)S(1)} copy-done((bf16[2,256,4,1024]{3,1,0,2:T(8,128)(2,1)S(1)}, bf16[2,256,4,1024]{3,1,0,2:T(8,128)(2,1)}, u32[]{:S(2)}) %copy-start) | copy-done | bytes 4194328
  20.9 14.2 %project.1 = f32[2,2,24,128]{3,2,1,0:T(8,128)S(1)} custom-call(bf16[4,2,256,1024]{3,2,1,0:T(8,128)(2,1)S(1)} %bitcast.7, bf16[2,1536,4096]{2,1,0:T(8,128)(2,1)} %bitcast.8, bf16[1,4096]{1,0:T(2,128)(2,1)S(1)} %reshape.14.weights_ref), custom_call_target="tpu_custom_call" | custom-call | flops 6442450944 | bytes 25165824 | tf_op jit(solution)/shard_map/project/pallas_call | solution.py:49
  35.1 0.6 reshape.15.part_ref
  35.7 35.8 %exchange.1 = f32[4,8,12,128]{3,2,1,0:T(8,128)} custom-call(f32[8,12,128]{2,1,0:T(8,128)} %reshape.15.part_ref), custom_call_target="tpu_custom_call" | custom-call | flops 1048576 | bytes 25165824 | tf_op jit(solution)/shard_map/exchange/pallas_call | solution.py:117
  71.6 1.6 %reshape_transpose_reshape.3.coef_ref = f32[8,2,24,128]{3,2,1,0:T(8,128)} reshape(f32[4,8,12,128]{3,2,1,0:T(8,128)} %exchange.1) | data formatting | bytes 393216 | tf_op jit(solution)/shard_map/reshape;transpose;reshape | solution.py:242
  73.2 0.0 all-to-all-done.modes_ref
  73.2 29.4 %synthesis.1 = f32[3200,1024]{1,0:T(8,128)} custom-call(f32[8,2,24,128]{3,2,1,0:T(8,128)} %reshape_transpose_reshape.3.coef_ref, bf16[4,2,256,1024]{3,2,1,0:T(8,128)(2,1)} %all-to-all-done.modes_ref, bf16[256,512]{1,0:T(8,128)(2,1)} %constant.3.basis_ref), custom_call_target="tpu_custom_call" | custom-call | flops 12884901888 | bytes 13107200 | tf_op jit(solution)/shard_map/synthesis/pallas_call | solution.py:201
  (1 shorter events, 0.0 us)
Async XLA Ops:
  13.4 5.3 %copy-start.1 = (bf16[4096]{0:T(1024)(128)(2,1)S(1)}, bf16[4096]{0:T(1024)(128)(2,1)}, u32[]{:S(2)}) copy-start(bf16[4096]{0:T(1024)(128)(2,1)} %param.6) | copy-start | bytes 24580
  13.4 59.9 %all-to-all-start = ((bf16[4,2,256,1024]{3,2,1,0:T(8,128)(2,1)}), bf16[4,2,256,1024]{3,2,1,0:T(8,128)(2,1)}, u32[]{:S(2)}, u32[]{:S(2)}) async-start(bf16[4,2,256,1024]{3,2,1,0:T(8,128)(2,1)} %bitcast.6), calls=%async_computation | async-start | bytes 8388608 | tf_op jit(solution)/shard_map/all_to_all | solution.py:232
  18.7 2.2 %copy-start = (bf16[2,256,4,1024]{3,1,0,2:T(8,128)(2,1)S(1)}, bf16[2,256,4,1024]{3,1,0,2:T(8,128)(2,1)}, u32[]{:S(2)}) copy-start(bf16[2,256,4,1024]{3,1,0,2:T(8,128)(2,1)} %copy.7) | copy-start | bytes 12582916
where the time goes:
time: 103 us
  Pallas kernels  79.4 us (77%)
  local copies, waits for them, and re-layouts  17.9 us (17%)
  starting transfers between devices  5.32 us (5%)
    pallas_call x1, Pallas kernels, exchange(): pl.pallas_call(functools.partial(exchange_kernel, n_freq, n_space), out_s...  35.8 us
    pallas_call x1, Pallas kernels, synthesis(): pl.pallas_call(functools.partial(synthesis_kernel, factor), out_shape=jax...  29.4 us
    pallas_call x1, Pallas kernels, project(): pl.pallas_call(functools.partial(project_kernel, blocks, group), out_shap...  14.2 us
    reshape x2, local copies, waits for them, and re-layouts, body(): eigvecs.reshape(2, count * modes_count, n_freq, width).transpose(2, 0, 1, 3)  13.4 us
    all_to_all x1, starting transfers between devices, body(): lax.all_to_all(send, 'freq', split_axis=0, concat_axis=0, tiled=True)  5.32 us
    unnamed x4, local copies, waits for them, and re-layouts  2.2 us
  transfers between devices with their start and end apart: 1, of which 0 were waited for; matrix products, arithmetic and copies ran while one was open for 2% of the time, Pallas kernels for 49%

commit v1 on v0

--- a/solution.py
+++ b/solution.py
@@ -9,16 +9,49 @@
 from jax.experimental.pallas import tpu as pltpu
 from jax.sharding import PartitionSpec as P
 
+
 MESH = pl.DeviceIdType.MESH
 GROUP = 32
 
 
-def project_kernel(blocks, group, modes_ref, spectra_ref, weights_ref, out_ref, acc_ref):
+def arrange_kernel(eigvecs_ref, *out_refs):
+    _, count, modes_count, width = eigvecs_ref.shape
+    rows = eigvecs_ref[0].reshape(count * modes_count, width)
+    start = 0
+    for out_ref in out_refs:
+        stop = start + out_ref.shape[3]
+        out_ref[0, 0] = rows[:, start:stop]
+        start = stop
+
+
+def arrange(eigvecs, parts, widths):
+    _, count, modes_count, points = eigvecs.shape
+    rows = count * modes_count
+    return pl.pallas_call(
+        arrange_kernel,
+        out_shape=[jax.ShapeDtypeStruct((parts, 2, rows, w), eigvecs.dtype) for w in widths],
+        grid=(parts, 2),
+        in_specs=[pl.BlockSpec((1, count, modes_count, points // parts), lambda d, c: (c, 0, 0, d))],
+        out_specs=[pl.BlockSpec((1, 1, rows, w), lambda d, c: (d, c, 0, 0)) for w in widths],
+        compiler_params=pltpu.CompilerParams(vmem_limit_bytes=62 << 20),
+        cost_estimate=pl.CostEstimate(flops=0, bytes_accessed=4 * eigvecs.size, transcendentals=0),
+        name="arrange",
+    )(eigvecs)
+
+
+def project_kernel(blocks, group, spectra_ref, weights_ref, *refs):
+    *modes_refs, out_ref, acc_ref = refs
     step = pl.program_id(1)
-    half = modes_ref.shape[2]
+    half = modes_refs[0].shape[2]
     weights = weights_ref[...].astype(jnp.float32)
     weighted = jnp.concatenate(
-        [(modes_ref[0, c].astype(jnp.float32) * weights).astype(jnp.bfloat16) for c in range(2)], axis=0
+        [
+            (
+                jnp.concatenate([ref[0, c] for ref in modes_refs], axis=1).astype(jnp.float32) * weights
+            ).astype(jnp.bfloat16)
+            for c in range(2)
+        ],
+        axis=0,
     )
     owner = lax.broadcasted_iota(jnp.int32, (blocks, 2 * half), 1) % half // (half // group)
 
@@ -42,7 +75,8 @@
 
 
 def project(modes, spectra, weights, blocks, group, modes_count):
-    parts, _, rows, width = modes.shape
+    parts, _, rows, _ = modes[0].shape
+    width = spectra.shape[2] // parts
     half = group * modes_count
     steps = rows // half
     points = spectra.shape[2]
@@ -51,20 +85,20 @@
         out_shape=jax.ShapeDtypeStruct((steps, 2, blocks, half), jnp.float32),
         grid=(steps, parts),
         in_specs=[
-            pl.BlockSpec((1, 2, half, width), lambda h, i: (i, 0, h, 0)),
             pl.BlockSpec((2, group * blocks, width), lambda h, i: (0, h, i)),
             pl.BlockSpec((1, width), lambda h, i: (0, i)),
-        ],
+        ]
+        + [pl.BlockSpec((1, 2, half, m.shape[3]), lambda h, i: (i, 0, h, 0)) for m in modes],
         out_specs=pl.BlockSpec((1, 2, blocks, half), lambda h, i: (h, 0, 0, 0)),
         scratch_shapes=[pltpu.VMEM((2, blocks, 2 * half), jnp.float32)],
-        compiler_params=pltpu.CompilerParams(vmem_limit_bytes=48 << 20),
+        compiler_params=pltpu.CompilerParams(vmem_limit_bytes=62 << 20),
         cost_estimate=pl.CostEstimate(
             flops=4 * spectra.shape[1] * points * 2 * half,
             bytes_accessed=4 * spectra.shape[1] * points,
             transcendentals=0,
         ),
         name="project",
-    )(modes, spectra, weights)
+    )(spectra, weights, *modes)
 
 
 def exchange_kernel(n_freq, n_space, part_ref, out_ref, land, own, every, send1, recv1, send2, recv2):
@@ -134,9 +168,10 @@
     )(part)
 
 
-def synthesis_kernel(factor, coef_ref, modes_ref, basis_ref, out_ref, left_ref, mid_ref):
+def synthesis_kernel(factor, coef_ref, modes_ref, basis_ref, *refs):
+    out_ref, left_ref, mid_ref = refs[-3:]
     groups, _, blocks, half = coef_ref.shape
-    parts, _, rows, tile = modes_ref.shape
+    _, _, rows, _ = modes_ref.shape
     chunk = 2 * GROUP
     length = groups * GROUP
 
@@ -186,38 +221,46 @@
     out_ref[blocks * step :] = carry
 
 
-def synthesis(coefs, modes, factor):
-    groups, _, blocks, half = coefs.shape
-    parts, _, rows, columns = modes.shape
+def basis_of(groups):
     length = groups * GROUP
-    tile = 256 if columns % 256 == 0 else columns
     freq = np.arange(length).reshape(groups, 1, GROUP)
     time = np.arange(length).reshape(length, 1, 1, 1)
     phase = 2.0 * np.pi * ((freq * time) % length) / length
     both = np.concatenate([np.cos(phase), -np.sin(phase)], axis=2)
     window = np.sin(np.pi * (np.arange(length) + 0.5) / length) / math.sqrt(length)
-    basis = jnp.asarray((both.reshape(length, 2 * length) * window[:, None]).astype(np.float32)).astype(jnp.bfloat16)
+    return jnp.asarray((both.reshape(length, 2 * length) * window[:, None]).astype(np.float32)).astype(jnp.bfloat16)
+
+
+def synthesis(coefs, modes, basis, factor, total, first, result):
+    groups, _, blocks, half = coefs.shape
+    parts, _, rows, columns = modes.shape
+    length = groups * GROUP
+    tile = 256 if columns % 256 == 0 else columns
+    offset = first // tile
     out_rows = (blocks + 1) * (length // 2)
+    earlier = [] if result is None else [result]
     return pl.pallas_call(
         functools.partial(synthesis_kernel, factor),
-        out_shape=jax.ShapeDtypeStruct((out_rows, columns), jnp.float32),
+        out_shape=jax.ShapeDtypeStruct((out_rows, total), jnp.float32),
         grid=(columns // tile,),
         in_specs=[
             pl.BlockSpec((groups, 2, blocks, half), lambda i: (0, 0, 0, 0)),
             pl.BlockSpec((parts, 2, rows, tile), lambda i: (0, 0, 0, i)),
             pl.BlockSpec((length, 2 * length), lambda i: (0, 0)),
-        ],
-        out_specs=pl.BlockSpec((out_rows, tile), lambda i: (0, i)),
+        ]
+        + [pl.BlockSpec(memory_space=pl.ANY) for _ in earlier],
+        out_specs=pl.BlockSpec((out_rows, tile), lambda i: (0, i + offset)),
+        input_output_aliases={3: 0} if earlier else {},
         scratch_shapes=[
             pltpu.VMEM((groups, blocks * 2 * GROUP, 2 * half), jnp.bfloat16),
             pltpu.VMEM((blocks, 2 * length, tile), jnp.bfloat16),
         ],
-        compiler_params=pltpu.CompilerParams(vmem_limit_bytes=56 << 20),
+        compiler_params=pltpu.CompilerParams(vmem_limit_bytes=40 << 20),
         cost_estimate=pl.CostEstimate(
             flops=8 * length * length * blocks * columns, bytes_accessed=4 * out_rows * columns, transcendentals=0
         ),
         name="synthesis",
-    )(coefs, modes, basis)
+    )(coefs, modes, basis, *earlier)
 
 
 def body(spectra, eigvecs, weights):
@@ -228,19 +271,32 @@
     factor = 1.0 / math.sqrt(points * n_space)
     group = min(GROUP, count)
     width = points // n_freq
-    send = eigvecs.reshape(2, count * modes_count, n_freq, width).transpose(2, 0, 1, 3)
-    moved = lax.all_to_all(send, "freq", split_axis=0, concat_axis=0, tiled=True)
-    part = project(
-        send, spectra.reshape(2, count * blocks, points), weights.reshape(1, points), blocks, group, modes_count
-    )
+    if width % 512 == 0:
+        widths = (width * 3 // 4, width // 4)
+    else:
+        widths = (width,)
+    send = arrange(eigvecs, n_freq, widths)
+    swap = functools.partial(lax.all_to_all, axis_name="freq", split_axis=0, concat_axis=0, tiled=True)
+    moved = [swap(send[0])]
+    spectra = spectra.reshape(2, count * blocks, points)
+    weights = weights.reshape(1, points)
+    part = project(send, spectra, weights, blocks, group, modes_count)
     piece = part.size // n_space
     shape = (piece // 128, 128) if piece % 128 == 0 else (1, piece)
-    coefs = exchange(part.reshape((n_space,) + shape), n_freq, n_space)
+    part = part.reshape((n_space,) + shape)
+    coefs = exchange(part, n_freq, n_space)
+    coefs, *later = lax.optimization_barrier((coefs, *send[1:]))
+    moved += [swap(block) for block in later]
     half = group * modes_count
     joined = GROUP // group
     coefs = coefs.reshape(-1, joined, 2, blocks, half).transpose(0, 2, 3, 1, 4)
     coefs = coefs.reshape(-1, 2, blocks, joined * half)
-    return synthesis(coefs, moved, factor)
+    basis = basis_of(coefs.shape[0])
+    result, first = None, 0
+    for block in moved:
+        result = synthesis(coefs, block, basis, factor, width, first, result)
+        first += block.shape[3]
+    return result
 
 
 def solution(mesh):

time: 103 us -> 90 us (0.87)
  local copies, waits for them, and re-layouts: 17.9 us -> 3.69 us
  starting transfers between devices: 5.32 us -> 8.72 us
  Pallas kernels: 79.4 us -> 77 us
    pallas_call x1, Pallas kernels: 35.8 us -> 23.7 us  [exchange(): pl.pallas_call(functools.partial(exchange_kernel, n_freq, n_space), out_s...]
    reshape x4 -> x2, local copies, waits for them, and re-layouts: 14 us -> 2.72 us  [the longest x1 1.42 us: body(): part = part.reshape((n_space,) + shape)]
    pallas_call x0 -> x1, Pallas kernels: none -> 6.65 us  [arrange(): pl.pallas_call(arrange_kernel, out_shape=[jax.ShapeDtypeStruct((parts, 2,...]
    all_to_all x1 -> x2, starting transfers between devices: 5.32 us -> 8.72 us  [the longest x1 5.19 us: body(): moved = [swap(send[0])]]
    pallas_call x1 -> x2, Pallas kernels: 29.4 us -> 31.6 us  [synthesis(): pl.pallas_call(functools.partial(synthesis_kernel, factor), out_shape=jax...]
    unnamed x4 -> x2, local copies, waits for them, and re-layouts: 2.2 us -> 0.01 us
  transfers between devices with their start and end apart: 1 -> 2, of which waited for: 0 -> 0; matrix products, arithmetic and copies ran while one was open for 2% -> 4% of each run, Pallas kernels for 49% -> 69%
where the time goes in v1:
time: 90 us; the launch traced here: 89.4 us
  Pallas kernels  77 us (86%)
  starting transfers between devices  8.72 us (10%)
  local copies, waits for them, and re-layouts  3.69 us (4%)
    pallas_call x2, Pallas kernels, synthesis(): pl.pallas_call(functools.partial(synthesis_kernel, factor), out_shape=jax...  31.6 us
    pallas_call x1, Pallas kernels, exchange(): pl.pallas_call(functools.partial(exchange_kernel, n_freq, n_space), out_s...  23.7 us
    pallas_call x1, Pallas kernels, project(): pl.pallas_call(functools.partial(project_kernel, blocks, group), out_shap...  15 us
    pallas_call x1, Pallas kernels, arrange(): pl.pallas_call(arrange_kernel, out_shape=[jax.ShapeDtypeStruct((parts, 2,...  6.65 us
    all_to_all x1, starting transfers between devices, body(): moved = [swap(send[0])]  5.19 us
    all_to_all x1, starting transfers between devices, body(): moved += [swap(block) for block in later]  3.53 us
  transfers between devices with their start and end apart: 2, of which 0 were waited for; matrix products, arithmetic and copies ran while one was open for 4% of the time, Pallas kernels for 69%

profile of v1, /device:TPU:0, one launch (start us, length us, event | category | flops | bytes accessed | tf_op | source)
XLA Modules:
  0.0 89.4 jit_solution(11920648205651390703)
XLA Ops:
  0.0 6.7 %arrange.1 = (bf16[4,2,256,768]{3,2,1,0:T(8,128)(2,1)}, bf16[4,2,256,256]{3,2,1,0:T(8,128)(2,1)}) custom-call(bf16[2,64,4,4096]{3,2,1,0:T(4,128)(2,1)} %eigvecs_ref.1), custom_call_target="tpu_custom_call" | custom-call | bytes 8388608 | tf_op jit(solution)/shard_map/arrange/pallas_call | solution.py:30
  6.7 5.2 %all-to-all-start.1 = ((bf16[4,2,256,768]{3,2,1,0:T(8,128)(2,1)}), bf16[4,2,256,768]{3,2,1,0:T(8,128)(2,1)}, u32[]{:S(2)}, u32[]{:S(2)}) async-start(bf16[4,2,256,768]{3,2,1,0:T(8,128)(2,1)} %get-tuple-element.9.refs_0_), calls=%async_computation.1 | async-start | bytes 6291456 | tf_op jit(solution)/shard_map/all_to_all | solution.py:280
  11.8 1.3 %reshape.10.weights_ref = bf16[1,4096]{1,0:T(2,128)(2,1)} reshape(bf16[4096]{0:T(1024)(128)(2,1)} %param.6) | data formatting | bytes 16384 | tf_op jit(solution)/shard_map/reshape | solution.py:282
  13.1 0.0 copy-start
  13.2 15.0 %project.1 = f32[2,2,24,128]{3,2,1,0:T(8,128)} custom-call(bf16[2,1536,4096]{2,1,0:T(8,128)(2,1)} %bitcast.3, bf16[1,4096]{1,0:T(2,128)(2,1)} %reshape.10.weights_ref, bf16[4,2,256,768]{3,2,1,0:T(8,128)(2,1)} %get-tuple-element.9.refs_0_, bf16[4,2,256,256]{3,2,1,0:T(8,128)(2,1)} %get-tuple-element.12.refs_1_), custom_call_target="tpu_custom_call" | custom-call | flops 6442450944 | bytes 25165824 | tf_op jit(solution)/shard_map/project/pallas_call | solution.py:83
  28.1 1.4 %reshape.11.part_ref = f32[8,12,128]{2,1,0:T(8,128)} reshape(f32[2,2,24,128]{3,2,1,0:T(8,128)} %project.1) | data formatting | bytes 98304 | tf_op jit(solution)/shard_map/reshape | solution.py:286
  29.5 23.7 %exchange.1 = f32[4,8,12,128]{3,2,1,0:T(8,128)} custom-call(f32[8,12,128]{2,1,0:T(8,128)} %reshape.11.part_ref), custom_call_target="tpu_custom_call" | custom-call | flops 1048576 | bytes 25165824 | tf_op jit(solution)/shard_map/exchange/pallas_call | solution.py:151
  53.3 1.0 %reshape_transpose_reshape.3.coef_ref = f32[8,2,24,128]{3,2,1,0:T(8,128)S(1)} reshape(f32[4,8,12,128]{3,2,1,0:T(8,128)} %exchange.1) | data formatting | bytes 393216 | tf_op jit(solution)/shard_map/reshape;transpose;reshape | solution.py:293
  54.2 0.0 all-to-all-done.1.modes_ref
  54.3 3.5 %all-to-all-start = ((bf16[4,2,256,256]{3,2,1,0:T(8,128)(2,1)}), bf16[4,2,256,256]{3,2,1,0:T(8,128)(2,1)S(1)}, u32[]{:S(2)}, u32[]{:S(2)}) async-start(bf16[4,2,256,256]{3,2,1,0:T(8,128)(2,1)} %get-tuple-element.12.refs_1_), calls=%async_computation | async-start | bytes 2097152 | tf_op jit(solution)/shard_map/all_to_all | solution.py:289
  57.8 0.0 copy-done
  57.8 22.8 %synthesis.2.refs_0_ = f32[3200,1024]{1,0:T(8,128)} custom-call(f32[8,2,24,128]{3,2,1,0:T(8,128)S(1)} %reshape_transpose_reshape.3.coef_ref, bf16[4,2,256,768]{3,2,1,0:T(8,128)(2,1)} %all-to-all-done.1.modes_ref, bf16[256,512]{1,0:T(8,128)(2,1)S(1)} %copy-done), custom_call_target="tpu_custom_call" | custom-call | flops 9663676416 | bytes 9830400 | tf_op jit(solution)/shard_map/synthesis/pallas_call | solution.py:242
  80.6 0.0 all-to-all-done.modes_ref
  80.6 8.8 %synthesis.3 = f32[3200,1024]{1,0:T(8,128)} custom-call(f32[8,2,24,128]{3,2,1,0:T(8,128)S(1)} %reshape_transpose_reshape.3.coef_ref, bf16[4,2,256,256]{3,2,1,0:T(8,128)(2,1)S(1)} %all-to-all-done.modes_ref, bf16[256,512]{1,0:T(8,128)(2,1)S(1)} %copy-done, f32[3200,1024]{1,0:T(8,128)} %synthesis.2.refs_0_), custom_call_target="tpu_custom_call", output_to_operand_aliasing={{}: (3, {})} | custom-call | flops 3221225472 | bytes 3276800 | tf_op jit(solution)/shard_map/synthesis/pallas_call | solution.py:242
Async XLA Ops:
  6.7 47.6 %all-to-all-start.1 = ((bf16[4,2,256,768]{3,2,1,0:T(8,128)(2,1)}), bf16[4,2,256,768]{3,2,1,0:T(8,128)(2,1)}, u32[]{:S(2)}, u32[]{:S(2)}) async-start(bf16[4,2,256,768]{3,2,1,0:T(8,128)(2,1)} %get-tuple-element.9.refs_0_), calls=%async_computation.1 | async-start | bytes 6291456 | tf_op jit(solution)/shard_map/all_to_all | solution.py:280
  13.1 44.6 %copy-start = (bf16[256,512]{1,0:T(8,128)(2,1)S(1)}, bf16[256,512]{1,0:T(8,128)(2,1)}, u32[]{:S(2)}) copy-start(bf16[256,512]{1,0:T(8,128)(2,1)} %constant.3.basis_ref) | copy-start | bytes 786436
  54.3 26.4 %all-to-all-start = ((bf16[4,2,256,256]{3,2,1,0:T(8,128)(2,1)}), bf16[4,2,256,256]{3,2,1,0:T(8,128)(2,1)S(1)}, u32[]{:S(2)}, u32[]{:S(2)}) async-start(bf16[4,2,256,256]{3,2,1,0:T(8,128)(2,1)} %get-tuple-element.12.refs_1_), calls=%async_computation | async-start | bytes 2097152 | tf_op jit(solution)/shard_map/all_to_all | solution.py:289
